TPU v7x, 32 devices: a whole 2x2x4 slice. The times are simulated.
32 devices in a mesh: lat: 16 (over z, y, x), field: 2 (over core).
Axes of the slice: x: 2, y: 2, z: 4, core: 2. Of those that a mesh axis runs over, the one named last changes fastest.
Arguments:
- fields_grid: bfloat16 [2, 64, 2, 48, 192], P('field', None, None, 'lat'), may hold values from -6 to 6
- basis: bfloat16 [128, 48, 96], P('lat'), may hold values from -0.875 to 0.875
- order_table: int32 [16, 8], replicated, may hold values from -1 to 95, as said below
- panel_modes: int32 [2, 64], replicated, may hold values from 0 to 95, as said below
Outputs:
- panel: bfloat16 [2, 128, 192, 128], P('field', 'lat')
Inputs may be any that keep to these rules, and one draw needn't show every extreme that they name: `order_table`: each order 0 to 95 stands in exactly one slot; every other slot holds -1; some group has all 8 slots filled. `panel_modes`: row 1 is never smaller than row 0 in the same column; degree 95 appears.
All inputs are finite; a program needn't handle non-finite values.
Results may differ from a plain program's by a relative error of at most 0.0082.
Values may be sent and summed in bfloat16 or wider, within the bound.
A program may use at most 64 MiB of HBM per device.

v0:
```python
import math
import jax
import jax.numpy as jnp
from jax import lax
from jax.sharding import PartitionSpec as P


def dft_table(orders, lon_count):
    valid_slot = orders >= 0
    safe_orders = jnp.maximum(orders, 0)
    products = lax.broadcasted_iota(jnp.int32, (lon_count, 1), 0) * safe_orders[None, :] % lon_count
    angles = products.astype(jnp.float32) * (2.0 * math.pi / lon_count)
    cosine = jnp.where(valid_slot[None, :], jnp.cos(angles), 0.0).astype(jnp.bfloat16)
    sine_table = jnp.where(valid_slot[None, :], -jnp.sin(angles), 0.0).astype(jnp.bfloat16)
    return jnp.stack([cosine, sine_table], axis=1)


def local(fields_grid, basis, order_table, panel_modes):
    grid_one = fields_grid[0]
    snap_count = grid_one.shape[0]
    pair_count = grid_one.shape[2]
    lon_count = grid_one.shape[3]
    slot_count = order_table.shape[1]
    deg_count = basis.shape[2]
    pair_total = basis.shape[1]
    mode_count = panel_modes.shape[1]
    orders = order_table.reshape(-1)
    slot_all = orders.shape[0]
    dft = dft_table(orders, lon_count)
    fourier = jnp.einsum("thjn,nrk->hkjrt", grid_one, dft, preferred_element_type=jnp.float32) * (
        1.0 / math.sqrt(lon_count)
    )
    fourier = fourier.reshape(2, slot_all, pair_count, 2 * snap_count)
    parity_parts = jnp.stack([fourier[0] + fourier[1], fourier[0] - fourier[1]]).astype(
        jnp.bfloat16
    )
    group_index = lax.axis_index("lat")
    my_orders = lax.dynamic_slice_in_dim(order_table, group_index, 1, 0)[0]
    my_odd = my_orders % 2 == 1
    basis_split = basis.reshape(slot_count, pair_total, deg_count // 2, 2)
    even_rows = basis_split[:, :, :, 0]
    odd_rows = basis_split[:, :, :, 1]
    degree = lax.broadcasted_iota(jnp.int32, (1, deg_count), 1)
    keep_mask = (degree >= my_orders[:, None]) & (my_orders >= 0)[:, None]
    received = lax.all_to_all(parity_parts, "lat", split_axis=1, concat_axis=2, tiled=True)
    first_parity = jnp.where(my_odd[:, None, None], received[1], received[0])
    second = jnp.where(my_odd[:, None, None], received[0], received[1])
    low_degrees = jnp.einsum(
        "sjh,sjc->shc", even_rows, first_parity, preferred_element_type=jnp.float32
    )
    high_degrees = jnp.einsum("sjh,sjc->shc", odd_rows, second, preferred_element_type=jnp.float32)
    joined = jnp.stack([low_degrees, high_degrees], axis=2).reshape(slot_count, deg_count, -1)
    coefficients = jnp.where(keep_mask[:, :, None], joined, 0.0).astype(jnp.bfloat16)
    mode_order = panel_modes[0]
    mode_degree = panel_modes[1]
    onehot = (my_orders[None, :] == mode_order[:, None]).astype(jnp.bfloat16)
    picked = jnp.take(coefficients, mode_degree, axis=1)
    local_values = jnp.einsum("ms,smc->mc", onehot, picked, preferred_element_type=jnp.float32)
    field_index = lax.axis_index("field")
    both_fields = jnp.stack(
        [
            jnp.where(field_index == 0, local_values, 0.0),
            jnp.where(field_index == 1, local_values, 0.0),
        ]
    )
    summed = lax.psum(both_fields, ("lat", "field"))
    other_field = jnp.where(field_index == 0, summed[1], summed[0]).astype(jnp.bfloat16)
    columns = other_field.astype(jnp.float32).reshape(mode_count * 2, snap_count)
    centered = (columns - jnp.mean(columns, axis=1, keepdims=True)).astype(jnp.bfloat16)
    coef_rows = coefficients.reshape(slot_count * deg_count * 2, snap_count)
    panel_values = lax.dot_general(
        coef_rows, centered, (((1,), (1,)), ((), ())), preferred_element_type=jnp.float32
    )
    panel_values = panel_values * (1.0 / (snap_count - 1))
    return panel_values.astype(jnp.bfloat16).reshape(1, slot_count, 2 * deg_count, 2 * mode_count)


def solution(mesh):
    placed = (P("field", None, None, "lat", None), P("lat", None, None), P(), P())
    return jax.shard_map(
        local, mesh=mesh, in_specs=placed, out_specs=P("field", "lat", None, None), check_vma=False
    )
```

profile of v0, /device:TPU:0, one launch (start us, length us, event | category | flops | bytes accessed | tf_op | source)
XLA Modules:
  0.0 63.5 jit_solution(17050038539362757233)
XLA Ops:
  0.0 0.0 copy-start.1
  0.0 0.8 %broadcast_compare_fusion = pred[16,8]{0,1:T(8,128)(4,1)S(1)} fusion(s32[16,8]{0,1:T(8,128)} %param.6), kind=kLoop, calls=%fused_computation.57 | loop fusion | flops 128 | bytes 640 | tf_op jit(solution)/shard_map/ge | solution.py:9
  0.8 0.0 copy-done.1
  0.8 0.1 copy.39
  0.9 0.1 ge.51
  1.0 0.1 copy.40
  1.0 0.1 max.11
  1.1 0.4 select_convert_fusion.1
  1.6 1.1 %fusion.1 = f32[2,128,3,2,64]{1,4,2,0,3:T(8,128)S(1)} fusion(bf16[64,2,3,192]{3,1,2,0:T(2,128)(2,1)} %bitcast.69, bf16[192,1,128]{2,0,1:T(8,128)(2,1)S(1)} %get-tuple-element.16, bf16[192,1,128]{2,0,1:T(8,128)(2,1)S(1)} %get-tuple-element.15), kind=kOutput, calls=%fused_computation.4 | convolution fusion | flops 38043648 | bytes 638976 | tf_op jit(solution)/shard_map/thjn,nrk->hkjrt/dot_general | solution.py:30
  2.8 0.8 %copy.44 = bf16[2,128,3,128]{3,0,2,1:T(2,128)(2,1)} copy(bf16[2,128,3,128]{1,3,2,0:T(8,128)(2,1)S(1)} %pad_maximum_fusion.1) | data formatting | bytes 393216 | tf_op jit(solution)/shard_map/stack | solution.py:34
  3.7 0.0 copy-start
  3.7 8.5 %all-to-all-start = ((bf16[2,128,3,128]{3,0,2,1:T(2,128)(2,1)}), bf16[2,128,3,128]{3,0,2,1:T(2,128)(2,1)S(1)}, u32[]{:S(2)}, u32[]{:S(2)}) async-start(bf16[2,128,3,128]{3,0,2,1:T(2,128)(2,1)} %copy.44), calls=%async_computation | async-start | bytes 393216 | tf_op jit(solution)/shard_map/all_to_all | solution.py:45
  12.1 0.0 copy-start.2
  12.2 0.7 %copy-done.2 = s32[2,64]{1,0:T(2,128)S(1)} copy-done((s32[2,64]{1,0:T(2,128)S(1)}, s32[2,64]{1,0:T(2,128)}, u32[]{:S(2)}) %copy-start.2) | copy-done | bytes 536
  12.8 0.2 dynamic-slice_reduce_fusion
  13.0 0.1 compare_bitcast_fusion
  13.2 0.0 copy-done
  13.2 0.2 copy.48
  13.4 7.4 %all-to-all-done = bf16[2,128,3,128]{3,0,2,1:T(2,128)(2,1)S(1)} async-done(((bf16[2,128,3,128]{3,0,2,1:T(2,128)(2,1)}), bf16[2,128,3,128]{3,0,2,1:T(2,128)(2,1)S(1)}, u32[]{:S(2)}, u32[]{:S(2)}) %all-to-all-start) | async-done | bytes 196640 | tf_op jit(solution)/shard_map/all_to_all | solution.py:45
  20.9 0.1 bitcast_select_fusion.2
  21.0 0.2 convolution_bitcast_fusion.1
  21.2 0.2 convolution_bitcast_fusion
  21.4 0.1 copy.53
  21.5 0.2 fusion.2
  21.7 0.6 gather_fusion
  22.3 0.3 fusion.5
  22.6 39.0 %psum.7 = bf16[2,64,128]{2,1,0:T(8,128)(2,1)S(1)} all-reduce(f32[2,64,128]{2,1,0:T(8,128)S(1)} %pad_maximum_fusion.2), channel_id=1, replica_groups=mesh['lat'=16,'field'=2] {'lat','field'}, use_global_device_ids=true, to_apply=%region_0.1 | all-reduce | flops 16384 | bytes 98304 | tf_op jit(solution)/shard_map/psum | solution.py:66
  61.6 0.1 reshape.345
  61.7 0.1 reduce_sum.9
  61.8 0.1 div.10
  62.0 0.1 sub.26
  62.1 0.1 sub.27
  62.2 0.1 convert_element_type.92
  62.3 0.2 convert_element_type.86
  62.5 1.0 %fusion = bf16[1536,128]{1,0:T(8,128)(2,1)} fusion(bf16[1536,64]{1,0:T(8,128)(2,1)S(1)} %convert_element_type.86, bf16[128,64]{1,0:T(8,128)(2,1)S(1)} %convert_element_type.92), kind=kOutput, calls=%fused_computation.2 | convolution fusion | flops 25559040 | bytes 606208 | tf_op jit(solution)/shard_map/dot_general | solution.py:71
  (23 shorter events, 0.3 us)
Async XLA Ops:
  0.0 0.8 %copy-start.1 = (s32[16,8]{0,1:T(8,128)S(1)}, s32[16,8]{0,1:T(8,128)}, u32[]{:S(2)}) copy-start(s32[16,8]{0,1:T(8,128)} %param.6) | copy-start | bytes 1540
  3.7 9.5 %copy-start = (bf16[8,48,96]{2,1,0:T(8,128)(2,1)S(1)}, bf16[8,48,96]{2,1,0:T(8,128)(2,1)}, u32[]{:S(2)}) copy-start(bf16[8,48,96]{2,1,0:T(8,128)(2,1)} %param.5) | copy-start | bytes 221188
  3.7 17.1 %all-to-all-start = ((bf16[2,128,3,128]{3,0,2,1:T(2,128)(2,1)}), bf16[2,128,3,128]{3,0,2,1:T(2,128)(2,1)S(1)}, u32[]{:S(2)}, u32[]{:S(2)}) async-start(bf16[2,128,3,128]{3,0,2,1:T(2,128)(2,1)} %copy.44), calls=%async_computation | async-start | bytes 393216 | tf_op jit(solution)/shard_map/all_to_all | solution.py:45
  12.1 0.7 %copy-start.2 = (s32[2,64]{1,0:T(2,128)S(1)}, s32[2,64]{1,0:T(2,128)}, u32[]{:S(2)}) copy-start(s32[2,64]{1,0:T(2,128)} %param.7) | copy-start | bytes 1540
where the time goes:
time: 63.9 us; the launch traced here: 63.5 us
  blocking collectives  39 us (61%)
  starting transfers between devices  8.47 us (13%)
  waiting for transfers between devices  7.41 us (12%)
  local copies, waits for them, and re-layouts  3.74 us (6%)
  matrix products  2.79 us (4%)
  other arithmetic  1.84 us (3%)
    psum x1, blocking collectives, local(): summed = lax.psum(both_fields, ('lat', 'field'))  39 us
    all_to_all x1, starting transfers between devices, local(): lax.all_to_all(parity_parts, 'lat', split_axis=1, concat_axis=2, tiled=True)  8.47 us
    all_to_all x1, waiting for transfers between devices, local(): lax.all_to_all(parity_parts, 'lat', split_axis=1, concat_axis=2, tiled=True)  7.41 us
  transfers between devices with their start and end apart: 1, of which 1 were waited for; matrix products, arithmetic and copies ran while one was open for 1% of the time, Pallas kernels for 0%

commit v1 on v0

--- a/solution.py
+++ b/solution.py
@@ -63,7 +63,9 @@
             jnp.where(field_index == 1, local_values, 0.0),
         ]
     )
-    summed = lax.psum(both_fields, ("lat", "field"))
+    summed = both_fields
+    for axis in ("field", "lat"):
+        summed = lax.psum(summed, axis)
     other_field = jnp.where(field_index == 0, summed[1], summed[0]).astype(jnp.bfloat16)
     columns = other_field.astype(jnp.float32).reshape(mode_count * 2, snap_count)
     centered = (columns - jnp.mean(columns, axis=1, keepdims=True)).astype(jnp.bfloat16)

time: 63.9 us -> 132 us (2.07)
  blocking collectives: 39 us -> 77.7 us
  waiting for transfers between devices: 7.41 us -> 22.8 us
  between operations: 0.28 us -> 13.6 us
    psum x1, blocking collectives: 39 us -> 77.7 us  [local(): summed = lax.psum(summed, axis)]
    psum x0 -> x1, waiting for transfers between devices: none -> 15.4 us  [local(): summed = lax.psum(summed, axis)]
  transfers between devices with their start and end apart: 1 -> 2, of which waited for: 1 -> 2; matrix products, arithmetic and copies ran while one was open for 1% -> 1% of each run, Pallas kernels for 0% -> 0%
where the time goes in v1:
time: 132 us
  blocking collectives  77.7 us (59%)
  waiting for transfers between devices  22.8 us (17%)
  between operations  13.6 us (10%)
  starting transfers between devices  8.51 us (6%)
  local copies, waits for them, and re-layouts  3.7 us (3%)
  matrix products  2.79 us (2%)
  other arithmetic  2.48 us (2%)
    psum x1, blocking collectives, local(): summed = lax.psum(summed, axis)  77.7 us
    psum x1, waiting for transfers between devices, local(): summed = lax.psum(summed, axis)  15.4 us
    all_to_all x1, starting transfers between devices, local(): lax.all_to_all(parity_parts, 'lat', split_axis=1, concat_axis=2, tiled=True)  8.47 us
    all_to_all x1, waiting for transfers between devices, local(): lax.all_to_all(parity_parts, 'lat', split_axis=1, concat_axis=2, tiled=True)  7.41 us
  transfers between devices with their start and end apart: 2, of which 2 were waited for; matrix products, arithmetic and copies ran while one was open for 1% of the time, Pallas kernels for 0%

profile of v1, /device:TPU:0, one launch (start us, length us, event | category | flops | bytes accessed | tf_op | source)
XLA Modules:
  0.0 131.7 jit_solution(16327015163990602540)
XLA Ops:
  6.5 0.0 copy-start.1
  6.5 0.8 broadcast_compare_fusion
  7.3 0.0 copy-done.1
  7.3 0.1 copy.39
  7.4 0.1 ge.51
  7.5 0.1 copy.40
  7.6 0.1 max.11
  7.7 0.4 select_convert_fusion.1
  8.1 1.1 fusion.1
  9.3 0.8 copy.44
  10.2 0.0 copy-start
  10.2 8.5 %all-to-all-start = ((bf16[2,128,3,128]{3,0,2,1:T(2,128)(2,1)}), bf16[2,128,3,128]{3,0,2,1:T(2,128)(2,1)S(1)}, u32[]{:S(2)}, u32[]{:S(2)}) async-start(bf16[2,128,3,128]{3,0,2,1:T(2,128)(2,1)} %copy.44), calls=%async_computation | async-start | bytes 393216 | tf_op jit(solution)/shard_map/all_to_all | solution.py:45
  18.7 0.0 copy-start.2
  18.7 0.0 all-reduce.2.cloned.1.call-start
  18.7 0.6 copy-done.2
  19.4 0.2 dynamic-slice_reduce_fusion
  19.6 0.1 compare_bitcast_fusion
  19.7 0.0 copy-done
  19.7 0.2 copy.48
  19.9 7.4 %all-to-all-done = bf16[2,128,3,128]{3,0,2,1:T(2,128)(2,1)S(1)} async-done(((bf16[2,128,3,128]{3,0,2,1:T(2,128)(2,1)}), bf16[2,128,3,128]{3,0,2,1:T(2,128)(2,1)S(1)}, u32[]{:S(2)}, u32[]{:S(2)}) %all-to-all-start) | async-done | bytes 196640 | tf_op jit(solution)/shard_map/all_to_all | solution.py:45
  27.4 0.1 bitcast_select_fusion.2
  27.5 0.2 convolution_bitcast_fusion.1
  27.7 0.2 convolution_bitcast_fusion
  27.9 0.1 copy.53
  28.0 0.2 fusion.2
  28.2 0.6 gather_fusion
  28.8 0.3 fusion.5
  29.1 0.6 pad_maximum_fusion.2
  29.7 0.0 all-reduce.2.cloned.1.call-update
  29.8 0.2 convert_element_type.86
  30.0 15.4 %all-reduce.2.cloned.1.call-done = f32[2,64,128]{2,1,0:T(8,128)} async-done(((f32[2,64,128]{2,1,0:T(8,128)}), f32[2,64,128]{2,1,0:T(8,128)}) %all-reduce.2.cloned.1.call-update) | async-done | bytes 65552 | tf_op jit(solution)/shard_map/psum | solution.py:68
  45.4 77.7 %psum.15 = bf16[2,64,128]{2,1,0:T(8,128)(2,1)S(1)} all-reduce(f32[2,64,128]{2,1,0:T(8,128)} %all-reduce.2.cloned.1.call-done), channel_id=1, replica_groups=mesh['lat'=16,'field'=2] {'lat'}, use_global_device_ids=true, to_apply=%region_1.2 | all-reduce | flops 16384 | bytes 98304 | tf_op jit(solution)/shard_map/psum | solution.py:68
  123.1 0.1 reshape.345
  123.2 0.1 reduce_sum.9
  123.3 0.1 div.10
  123.5 0.1 sub.26
  123.6 0.1 sub.27
  123.7 0.1 convert_element_type.92
  123.8 1.0 fusion
  (22 shorter events, 0.3 us)
Async XLA Ops:
  6.5 0.8 copy-start.1
  10.2 9.5 %copy-start = (bf16[8,48,96]{2,1,0:T(8,128)(2,1)S(1)}, bf16[8,48,96]{2,1,0:T(8,128)(2,1)}, u32[]{:S(2)}) copy-start(bf16[8,48,96]{2,1,0:T(8,128)(2,1)} %param.5) | copy-start | bytes 221188
  10.2 17.1 %all-to-all-start = ((bf16[2,128,3,128]{3,0,2,1:T(2,128)(2,1)}), bf16[2,128,3,128]{3,0,2,1:T(2,128)(2,1)S(1)}, u32[]{:S(2)}, u32[]{:S(2)}) async-start(bf16[2,128,3,128]{3,0,2,1:T(2,128)(2,1)} %copy.44), calls=%async_computation | async-start | bytes 393216 | tf_op jit(solution)/shard_map/all_to_all | solution.py:45
  18.7 0.7 copy-start.2
  18.7 26.7 %all-reduce.2.cloned.1.call-start = ((), (), s32[]{:S(2)}) async-start(), calls=%async_computation.1 | async-start | bytes 131072 | tf_op jit(solution)/shard_map/psum | solution.py:68
Sparse Core Ops, SparseCore 0:
  29.9 15.4 all-reduce.1
